TPU v7x, 32 devices: a whole 2x2x4 slice. The times are simulated.
32 devices in a mesh: dp: 2 (over y), row: 4 (over x, core), col: 4 (over z).
Axes of the slice: x: 2, y: 2, z: 4, core: 2. Of those that a mesh axis runs over, the one named last changes fastest.
Arguments:
- tokens: bfloat16 [1024, 1024], P(('dp', 'row'), 'col'), may hold values from -12 to 12
- cotangent: bfloat16 [1024, 1024], P(('dp', 'row'), 'col'), may hold values from -6 to 6
- first_gain: float32 [1024], P('col'), may hold values from 0.25 to 1.75
- first_shift: float32 [1024], P('col'), may hold values from -3 to 3
- w_qkv: bfloat16 [1024, 3072], P('col', 'row'), may hold values from -0.1875 to 0.1875
- bias_qv: float32 [2048], P('row'), may hold values from -4 to 4
- w_out: bfloat16 [1024, 1024], P('row', 'col'), may hold values from -0.375 to 0.375
- bias_out: float32 [1024], P('col'), may hold values from -3 to 3
- second_gain: float32 [1024], P('col'), may hold values from 0.25 to 1.75
- second_shift: float32 [1024], P('col'), may hold values from -3 to 3
- w_up: bfloat16 [1024, 4096], P('col', 'row'), may hold values from -0.1875 to 0.1875
- bias_up: float32 [4096], P('row'), may hold values from -4 to 4
- w_down: bfloat16 [4096, 1024], P('row', 'col'), may hold values from -0.125 to 0.125
- bias_down: float32 [1024], P('col'), may hold values from -3 to 3
Outputs:
- block_out: bfloat16 [1024, 1024], P(('dp', 'row'), 'col')
- grad_tokens: float32 [1024, 1024], P(('dp', 'row'), 'col')
- grad_first_gain: float32 [1024], P('col')
- grad_first_shift: float32 [1024], P('col')
- grad_w_qkv: float32 [1024, 3072], P('col', 'row')
- grad_bias_qv: float32 [2048], P('row')
- grad_w_out: float32 [1024, 1024], P('row', 'col')
- grad_bias_out: float32 [1024], P('col')
- grad_second_gain: float32 [1024], P('col')
- grad_second_shift: float32 [1024], P('col')
- grad_w_up: float32 [1024, 4096], P('col', 'row')
- grad_bias_up: float32 [4096], P('row')
- grad_w_down: float32 [4096, 1024], P('row', 'col')
- grad_bias_down: float32 [1024], P('col')
All inputs are finite; a program needn't handle non-finite values.
Results may differ from a plain program's by a relative error of at most 0.012.
Values may be sent and summed in bfloat16 or wider, within the bound.
No kernel may reach another device: no remote copies, remote signals or barrier semaphores. Data moves between devices by JAX's collectives and lax.ppermute only.
A program may use at most 64 MiB of HBM per device.

v0:
```python
import jax
import jax.numpy as jnp
from jax import lax
from jax.sharding import PartitionSpec as P

HEADS = 16
HEAD_DIM = 64
SEQ = 512
EPS = 1e-05
GELU_C = 0.7978845608028654
GELU_A = 0.044715


def gelu_pair(hidden):
    inner = GELU_C * (hidden + GELU_A * hidden * hidden * hidden)
    tanh_val = jnp.tanh(inner)
    value = 0.5 * hidden * (1.0 + tanh_val)
    slope = 0.5 * (1.0 + tanh_val) + 0.5 * hidden * (1.0 - tanh_val * tanh_val) * GELU_C * (
        1.0 + 3.0 * GELU_A * hidden * hidden
    )
    return (value, slope)


def feature_stats(first_part, second_part):
    return lax.psum((first_part, second_part), "col")


def normalize(matrix, gain, shift):
    width = matrix.shape[1] * lax.axis_size("col")
    total_one, total_two = feature_stats(jnp.sum(matrix, 1), jnp.sum(matrix * matrix, 1))
    centre = total_one / width
    spread = total_two / width - centre * centre
    rstd = lax.rsqrt(spread + EPS)[:, None]
    normed = (matrix - centre[:, None]) * rstd
    return (normed, rstd, (normed * gain + shift).astype(jnp.bfloat16))


def normalize_back(grad, normed, rstd, gain):
    width = grad.shape[1] * lax.axis_size("col")
    scaled = grad * gain
    total_one, total_two = feature_stats(jnp.sum(scaled, 1), jnp.sum(scaled * normed, 1))
    return rstd * (scaled - total_one[:, None] / width - normed * (total_two[:, None] / width))


def product(left, matrix, transposed):
    if transposed:
        return lax.dot_general(
            left, matrix, (((1,), (1,)), ((), ())), preferred_element_type=jnp.float32
        )
    return jnp.dot(left, matrix, preferred_element_type=jnp.float32)


def outer_grad(left, right):
    return lax.dot_general(
        left, right, (((0,), (0,)), ((), ())), preferred_element_type=jnp.float32
    )


def rows_in(block):
    return lax.all_gather(block, "row", axis=0, tiled=True)


def cols_in(block):
    return lax.all_gather(block, "col", axis=0, tiled=True)


def to_cols(whole, matrix, transposed):
    own_rows = whole.shape[0] // lax.axis_size("col")

    def term(first_row, row_count):
        return product(whole, matrix, transposed)

    return lax.psum_scatter(
        term(jnp.int32(0), lax.axis_size("col") * own_rows), "col", scatter_dimension=0, tiled=True
    )


def to_rows(whole, matrix, transposed):
    own_rows = whole.shape[0] // lax.axis_size("row")

    def term(first_row, row_count):
        return product(whole, matrix, transposed)

    return lax.psum_scatter(
        term(jnp.int32(0), lax.axis_size("row") * own_rows), "row", scatter_dimension=0, tiled=True
    )


def block_scores(query_block, query_pos, keys_all, slopes):
    key_pos = jnp.arange(keys_all.shape[0], dtype=jnp.int32)
    offsets = query_pos[:, None] - key_pos[None, :]
    causal_mask = (offsets >= 0) & (query_pos[:, None] // SEQ == key_pos[None, :] // SEQ)
    scores = (
        jnp.einsum("qhe,khe->hqk", query_block, keys_all, preferred_element_type=jnp.float32)
        * 0.125
    )
    scores = scores - slopes[:, None, None] * offsets.astype(jnp.float32)[None]
    return jnp.where(causal_mask[None], scores, -30000.0)


def local(
    tokens,
    cotangent,
    first_gain,
    first_shift,
    w_qkv,
    bias_qv,
    w_out,
    bias_out,
    second_gain,
    second_shift,
    w_up,
    bias_up,
    w_down,
    bias_down,
):
    rows_a = tokens.shape[0]
    group_rows = rows_a * lax.axis_size("row")
    rows_b = group_rows // lax.axis_size("col")
    head_count = bias_qv.shape[0] // (2 * HEAD_DIM)
    head_ids = lax.axis_index("row") * head_count + jnp.arange(head_count, dtype=jnp.int32)
    slopes = jnp.exp2(-8.0 * (head_ids.astype(jnp.float32) + 1.0) / HEADS)
    query_pos = lax.axis_index("col") * rows_b + jnp.arange(rows_b, dtype=jnp.int32)
    block_rows = min(rows_b, 512)
    block_count = rows_b // block_rows
    inputs_f = tokens.astype(jnp.float32)
    normed_one, rstd_one, first_in = normalize(inputs_f, first_gain, first_shift)
    first_all = rows_in(first_in)
    joined = to_cols(first_all, w_qkv, False).reshape(rows_b, head_count, 3, HEAD_DIM)
    bias_pair = bias_qv.reshape(head_count, 2, HEAD_DIM)
    queries = (joined[:, :, 0] + bias_pair[:, 0]).astype(jnp.bfloat16)
    keys_here = joined[:, :, 1].astype(jnp.bfloat16)
    values_here = (joined[:, :, 2] + bias_pair[:, 1]).astype(jnp.bfloat16)
    keys_flat, values_flat = (
        lax.all_gather(keys_here.reshape(rows_b, -1), "col", axis=0, tiled=True),
        lax.all_gather(values_here.reshape(rows_b, -1), "col", axis=0, tiled=True),
    )
    keys_all = keys_flat.reshape(group_rows, head_count, HEAD_DIM)
    values_all = values_flat.reshape(group_rows, head_count, HEAD_DIM)
    query_blocks = queries.reshape(block_count, block_rows, head_count, HEAD_DIM)
    pos_blocks = query_pos.reshape(block_count, block_rows)

    def forward_block(inputs):
        query_block, block_pos = inputs
        scores = block_scores(query_block, block_pos, keys_all, slopes)
        exponent = jnp.exp(scores)
        row_total = jnp.sum(exponent, -1)
        numerator = jnp.einsum(
            "hqk,khe->qhe",
            exponent.astype(jnp.bfloat16),
            values_all,
            preferred_element_type=jnp.float32,
        )
        context_block = (numerator / row_total.T[:, :, None]).astype(jnp.bfloat16)
        return (context_block, jnp.log(row_total))

    context_blocks, logsum_blocks = lax.map(forward_block, (query_blocks, pos_blocks))
    context = context_blocks.reshape(rows_b, head_count * HEAD_DIM)
    context_all = cols_in(context)
    resid = inputs_f + to_rows(context_all, w_out, False) + bias_out
    normed_two, rstd_two, second_in = normalize(resid, second_gain, second_shift)
    second_all = rows_in(second_in)
    pre_act = to_cols(second_all, w_up, False) + bias_up
    act, slope_act = gelu_pair(pre_act)
    act_all = cols_in(act.astype(jnp.bfloat16))
    block_out = (resid + to_rows(act_all, w_down, False) + bias_down).astype(jnp.bfloat16)
    cot_f = cotangent.astype(jnp.float32)
    cot_all = rows_in(cotangent)
    grad_down = outer_grad(act_all, cot_all)
    grad_pre = to_cols(cot_all, w_down, True) * slope_act
    up_bias_part = jnp.sum(grad_pre, 0)
    grad_pre_all = cols_in(grad_pre.astype(jnp.bfloat16))
    grad_up = outer_grad(second_all, grad_pre_all)
    grad_second = to_rows(grad_pre_all, w_up, True)
    second_gain_part = jnp.sum(grad_second * normed_two, 0)
    second_shift_part = jnp.sum(grad_second, 0)
    grad_resid = cot_f + normalize_back(grad_second, normed_two, rstd_two, second_gain)
    out_bias_part = jnp.sum(grad_resid, 0)
    down_bias_part = jnp.sum(cot_f, 0)
    resid_all = rows_in(grad_resid.astype(jnp.bfloat16))
    grad_out = outer_grad(context_all, resid_all)
    grad_context = to_cols(resid_all, w_out, True).astype(jnp.bfloat16)
    grad_ctx_blocks = grad_context.reshape(block_count, block_rows, head_count, HEAD_DIM)

    def backward_block(running, inputs):
        key_acc, value_acc = running
        query_block, block_pos, context_block, grad_block, logsum_block = inputs
        scores = block_scores(query_block, block_pos, keys_all, slopes)
        probs = jnp.exp(scores - logsum_block[:, :, None])
        delta = jnp.sum(grad_block.astype(jnp.float32) * context_block.astype(jnp.float32), -1).T
        dprob = jnp.einsum(
            "qhe,khe->hqk", grad_block, values_all, preferred_element_type=jnp.float32
        )
        dscore = (probs * (dprob - delta[:, :, None])).astype(jnp.bfloat16)
        grad_q = (
            jnp.einsum("hqk,khe->qhe", dscore, keys_all, preferred_element_type=jnp.float32) * 0.125
        )
        key_acc = (
            key_acc
            + jnp.einsum("hqk,qhe->khe", dscore, query_block, preferred_element_type=jnp.float32)
            * 0.125
        )
        value_acc = value_acc + jnp.einsum(
            "hqk,qhe->khe",
            probs.astype(jnp.bfloat16),
            grad_block,
            preferred_element_type=jnp.float32,
        )
        return ((key_acc, value_acc), grad_q)

    empty = jnp.zeros((group_rows, head_count, HEAD_DIM), jnp.float32)
    (key_acc, value_acc), grad_q_blocks = lax.scan(
        backward_block,
        (empty, empty),
        (query_blocks, pos_blocks, context_blocks, grad_ctx_blocks, logsum_blocks),
    )
    grad_k, grad_v = (
        lax.psum_scatter(key_acc.reshape(group_rows, -1), "col", scatter_dimension=0, tiled=True),
        lax.psum_scatter(value_acc.reshape(group_rows, -1), "col", scatter_dimension=0, tiled=True),
    )
    grad_q = grad_q_blocks.reshape(rows_b, head_count, HEAD_DIM)
    grad_k = grad_k.reshape(rows_b, head_count, HEAD_DIM)
    grad_v = grad_v.reshape(rows_b, head_count, HEAD_DIM)
    grad_joined = jnp.stack([grad_q, grad_k, grad_v], 2)
    qv_bias_part = jnp.sum(jnp.stack([grad_q, grad_v], 2), 0).reshape(-1)
    joined_all = cols_in(grad_joined.reshape(rows_b, -1).astype(jnp.bfloat16))
    grad_qkv = outer_grad(first_all, joined_all)
    grad_first = to_rows(joined_all, w_qkv, True)
    first_gain_part = jnp.sum(grad_first * normed_one, 0)
    first_shift_part = jnp.sum(grad_first, 0)
    grad_tokens = grad_resid + normalize_back(grad_first, normed_one, rstd_one, first_gain)
    grad_qkv, grad_out, grad_up, grad_down = lax.psum(
        (grad_qkv, grad_out, grad_up, grad_down), "dp"
    )
    gain_one, shift_one, gain_two, shift_two, out_bias_grad, down_bias_grad = lax.psum(
        (
            first_gain_part,
            first_shift_part,
            second_gain_part,
            second_shift_part,
            out_bias_part,
            down_bias_part,
        ),
        ("dp", "row"),
    )
    qv_bias_grad, up_bias_grad = lax.psum((qv_bias_part, up_bias_part), ("dp", "col"))
    return (
        block_out,
        grad_tokens,
        gain_one,
        shift_one,
        grad_qkv,
        qv_bias_grad,
        grad_out,
        out_bias_grad,
        gain_two,
        shift_two,
        grad_up,
        up_bias_grad,
        grad_down,
        down_bias_grad,
    )


def solution(mesh):
    placed = (
        P(("dp", "row"), "col"),
        P(("dp", "row"), "col"),
        P("col"),
        P("col"),
        P("col", "row"),
        P("row"),
        P("row", "col"),
        P("col"),
        P("col"),
        P("col"),
        P("col", "row"),
        P("row"),
        P("row", "col"),
        P("col"),
    )
    return jax.shard_map(
        local,
        mesh=mesh,
        in_specs=placed,
        out_specs=(
            P(("dp", "row"), "col"),
            P(("dp", "row"), "col"),
            P("col"),
            P("col"),
            P("col", "row"),
            P("row"),
            P("row", "col"),
            P("col"),
            P("col"),
            P("col"),
            P("col", "row"),
            P("row"),
            P("row", "col"),
            P("col"),
        ),
        check_vma=False,
    )
```

profile of v0, /device:TPU:0, one launch (start us, length us, event | category | flops | bytes accessed | tf_op | source)
XLA Modules:
  0.0 548.3 jit_solution(9419298570931146965)
XLA Ops:
  8.2 13.5 %all-reduce.5 = (f32[128]{0:T(128)S(1)}, f32[128]{0:T(128)S(1)}) all-reduce(f32[128]{0:T(128)S(1)} %get-tuple-element.85, f32[128]{0:T(128)S(1)} %get-tuple-element.84), channel_id=1, replica_groups=mesh['dp'=2,'row'=4,'col'=4] {'col'}, use_global_device_ids=true, to_apply=%region_3.0 | all-reduce | flops 256 | bytes 2048 | tf_op jit(solution)/shard_map/psum | solution.py:25
  22.7 5.8 %all_gather.30 = bf16[512,256]{1,0:T(8,128)(2,1)S(1)} all-gather(bf16[128,256]{1,0:T(8,128)(2,1)S(1)} %fusion.26), channel_id=1, replica_groups=mesh['dp'=2,'row'=4,'col'=4] {'row'}, dimensions={0}, use_global_device_ids=true | all-gather | bytes 327680 | tf_op jit(solution)/shard_map/all_gather | solution.py:60
  29.2 2.5 fusion.49
  32.3 33.3 %reduce-scatter.11.cloned.1.call-done = f32[128,768]{1,0:T(8,128)} async-done(((f32[512,768]{1,0:T(8,128)}), f32[128,768]{1,0:T(8,128)}) %reduce-scatter.11.cloned.1.call-update) | async-done | bytes 393232 | tf_op jit(solution)/shard_map/reduce_scatter | solution.py:73
  66.9 13.4 %all_gather.31 = bf16[512,256]{0,1:T(8,128)(2,1)S(1)} all-gather(bf16[128,256]{0,1:T(8,128)(2,1)S(1)} %fusion.36), channel_id=1, replica_groups=mesh['dp'=2,'row'=4,'col'=4] {'col'}, dimensions={0}, use_global_device_ids=true | all-gather | bytes 327680 | tf_op jit(solution)/shard_map/all_gather | solution.py:136
  80.2 13.2 %all_gather.32 = bf16[512,256]{0,1:T(8,128)(2,1)S(1)} all-gather(bf16[128,256]{0,1:T(8,128)(2,1)S(1)} %bitcast.91), channel_id=1, replica_groups=mesh['dp'=2,'row'=4,'col'=4] {'col'}, dimensions={0}, use_global_device_ids=true | all-gather | bytes 327680 | tf_op jit(solution)/shard_map/all_gather | solution.py:135
  94.5 12.8 %all_gather.33 = bf16[512,256]{0,1:T(8,128)(2,1)S(1)} all-gather(bf16[128,256]{0,1:T(8,128)(2,1)S(1)} %bitcast.89), channel_id=1, replica_groups=mesh['dp'=2,'row'=4,'col'=4] {'col'}, dimensions={0}, use_global_device_ids=true | all-gather | bytes 327680 | tf_op jit(solution)/shard_map/all_gather | solution.py:64
  109.1 5.8 %all_gather.36 = bf16[512,256]{1,0:T(8,128)(2,1)S(1)} all-gather(bf16[128,256]{1,0:T(8,128)(2,1)S(1)} %copy-done.21), channel_id=1, replica_groups=mesh['dp'=2,'row'=4,'col'=4] {'row'}, dimensions={0}, use_global_device_ids=true | all-gather | bytes 327680 | tf_op jit(solution)/shard_map/all_gather | solution.py:60
  117.6 11.7 %reduce-scatter.13.cloned.1.call-done = f32[128,256]{1,0:T(8,128)} async-done(((f32[512,256]{1,0:T(8,128)}), f32[128,256]{1,0:T(8,128)}) %reduce-scatter.13.cloned.1.call-update) | async-done | bytes 131088 | tf_op jit(solution)/shard_map/reduce_scatter | solution.py:84
  130.2 11.8 %all-reduce.4 = (f32[128]{0:T(128)S(1)}, f32[128]{0:T(128)S(1)}) all-reduce(f32[128]{0:T(128)S(1)} %get-tuple-element.83, f32[128]{0:T(128)S(1)} %get-tuple-element.82), channel_id=1, replica_groups=mesh['dp'=2,'row'=4,'col'=4] {'col'}, use_global_device_ids=true, to_apply=%region_10.11 | all-reduce | flops 256 | bytes 2048 | tf_op jit(solution)/shard_map/psum | solution.py:25
  142.2 5.8 %all_gather.34 = bf16[512,256]{1,0:T(8,128)(2,1)S(1)} all-gather(bf16[128,256]{1,0:T(8,128)(2,1)S(1)} %add_convert_fusion.1), channel_id=1, replica_groups=mesh['dp'=2,'row'=4,'col'=4] {'row'}, dimensions={0}, use_global_device_ids=true | all-gather | bytes 327680 | tf_op jit(solution)/shard_map/all_gather | solution.py:60
  150.5 24.8 %reduce-scatter.19.cloned.1.call-done = f32[128,1024]{1,0:T(8,128)} async-done(((f32[512,1024]{1,0:T(8,128)}), f32[128,1024]{1,0:T(8,128)}) %reduce-scatter.19.cloned.1.call-update) | async-done | bytes 524304 | tf_op jit(solution)/shard_map/reduce_scatter | solution.py:73
  175.2 44.9 %reduce-scatter.15.cloned.1.call-done = f32[128,1024]{1,0:T(8,128)} async-done(((f32[512,1024]{1,0:T(8,128)}), f32[128,1024]{1,0:T(8,128)}) %reduce-scatter.15.cloned.1.call-update) | async-done | bytes 524304 | tf_op jit(solution)/shard_map/reduce_scatter | solution.py:73
  220.1 2.4 fusion.43
  223.2 26.7 %all-gather.5.cloned.1.call-done = bf16[512,1024]{1,0:T(8,128)(2,1)} async-done(((bf16[128,1024]{1,0:T(8,128)(2,1)}), bf16[512,1024]{1,0:T(8,128)(2,1)}) %all-gather.5.cloned.1.call-update) | async-done | bytes 1048592 | tf_op jit(solution)/shard_map/all_gather | solution.py:64
  249.9 2.5 fusion.54
  252.5 26.8 %all-gather.3.cloned.1.call-done = bf16[512,1024]{1,0:T(8,128)(2,1)} async-done(((bf16[128,1024]{1,0:T(8,128)(2,1)}), bf16[512,1024]{1,0:T(8,128)(2,1)}) %all-gather.3.cloned.1.call-update) | async-done | bytes 1048592 | tf_op jit(solution)/shard_map/all_gather | solution.py:64
  279.3 2.5 fusion.52
  281.8 21.6 %reduce-scatter.21.cloned.1.call-done = f32[128,256]{1,0:T(8,128)} async-done(((f32[512,256]{1,0:T(8,128)}), f32[128,256]{1,0:T(8,128)}) %reduce-scatter.21.cloned.1.call-update) | async-done | bytes 131088 | tf_op jit(solution)/shard_map/reduce_scatter | solution.py:84
  304.5 11.7 %all-reduce.3 = (f32[128]{0:T(128)S(1)}, f32[128]{0:T(128)S(1)}) all-reduce(f32[128]{0:T(128)S(1)} %get-tuple-element.63, f32[128]{0:T(128)S(1)} %get-tuple-element.67), channel_id=1, replica_groups=mesh['dp'=2,'row'=4,'col'=4] {'col'}, use_global_device_ids=true, to_apply=%region_18.19 | all-reduce | flops 256 | bytes 2048 | tf_op jit(solution)/shard_map/psum | solution.py:25
  316.2 12.0 %reduce-scatter.17.cloned.1.call-done = f32[128,256]{1,0:T(8,128)} async-done(((f32[512,256]{1,0:T(8,128)}), f32[128,256]{1,0:T(8,128)}) %reduce-scatter.17.cloned.1.call-update) | async-done | bytes 131088 | tf_op jit(solution)/shard_map/reduce_scatter | solution.py:84
  329.8 5.8 %all_gather.38 = bf16[512,256]{1,0:T(8,128)(2,1)S(1)} all-gather(bf16[128,256]{1,0:T(8,128)(2,1)S(1)} %convert_element_type.98), channel_id=1, replica_groups=mesh['dp'=2,'row'=4,'col'=4] {'row'}, dimensions={0}, use_global_device_ids=true | all-gather | bytes 327680 | tf_op jit(solution)/shard_map/all_gather | solution.py:60
  337.4 21.9 %reduce-scatter.23.cloned.1.call-done = f32[128,256]{1,0:T(8,128)} async-done(((f32[512,256]{1,0:T(8,128)}), f32[128,256]{1,0:T(8,128)}) %reduce-scatter.23.cloned.1.call-update) | async-done | bytes 131088 | tf_op jit(solution)/shard_map/reduce_scatter | solution.py:73
  364.1 18.0 %reduce-scatter.27.cloned.1.call-done = f32[128,256]{0,1:T(8,128)} async-done(((f32[512,256]{0,1:T(8,128)}), f32[128,256]{0,1:T(8,128)}) %reduce-scatter.27.cloned.1.call-update) | async-done | bytes 131088 | tf_op jit(solution)/shard_map/reduce_scatter | solution.py:219
  383.0 22.0 %reduce-scatter.25.cloned.1.call-done = f32[128,256]{0,1:T(8,128)} async-done(((f32[512,256]{0,1:T(8,128)}), f32[128,256]{0,1:T(8,128)}) %reduce-scatter.25.cloned.1.call-update) | async-done | bytes 131088 | tf_op jit(solution)/shard_map/reduce_scatter | solution.py:218
  405.9 17.0 %all_gather.39 = bf16[512,768]{0,1:T(8,128)(2,1)S(1)} all-gather(bf16[128,768]{0,1:T(8,128)(2,1)S(1)} %bitcast.88), channel_id=1, replica_groups=mesh['dp'=2,'row'=4,'col'=4] {'col'}, dimensions={0}, use_global_device_ids=true | all-gather | bytes 983040 | tf_op jit(solution)/shard_map/all_gather | solution.py:64
  422.9 2.3 fusion.56
  425.3 2.4 fusion.59
  431.8 20.6 %all-reduce = (f32[512]{0:T(512)}, f32[1024]{0:T(1024)}) all-reduce(f32[512]{0:T(512)S(1)} %reshape.258, f32[1024]{0:T(1024)S(1)} %get-tuple-element.106), channel_id=1, replica_groups=mesh['dp'=2,'row'=4,'col'=4] {'dp','col'}, use_global_device_ids=true, to_apply=%region_34.35 | all-reduce | flops 1536 | bytes 12288 | tf_op jit(solution)/shard_map/psum | solution.py:246
  453.4 8.4 %all-reduce.2 = (f32[128]{0:T(128)S(1)}, f32[128]{0:T(128)S(1)}) all-reduce(f32[128]{0:T(128)S(1)} %get-tuple-element.65, f32[128]{0:T(128)S(1)} %get-tuple-element.66), channel_id=1, replica_groups=mesh['dp'=2,'row'=4,'col'=4] {'col'}, use_global_device_ids=true, to_apply=%region_27.28 | all-reduce | flops 256 | bytes 2048 | tf_op jit(solution)/shard_map/psum | solution.py:25
  461.8 13.0 %all-reduce.1 = (f32[256]{0:T(256)}, f32[256]{0:T(256)}, f32[256]{0:T(256)}, f32[256]{0:T(256)}, f32[256]{0:T(256)}, /*index=5*/f32[256]{0:T(256)}) all-reduce(f32[256]{0:T(256)S(1)} %get-tuple-element.64, f32[256]{0:T(256)S(1)} %get-tuple-element.81, ...), channel_id=1, replica_groups=mesh['dp'=2,'row'=4,'col'=4] {'dp','row'}, use_global_device_ids=true, to_apply=%region_29.30 | all-reduce | flops 1536 | bytes 12288 | tf_op jit(solution)/shard_map/psum | solution.py:235
  476.5 59.5 %all-reduce.9.cloned.1.call-done = (f32[256,768]{1,0:T(8,128)}, f32[256,256]{1,0:T(8,128)}, f32[256,1024]{1,0:T(8,128)}, f32[1024,256]{1,0:T(8,128)}) async-done(((f32[256,768]{1,0:T(8,128)}, f32[256,256]{1,0:T(8,128)}, f32[256,1024]{1,0:T(8,128)}, f32[1024,256]{1,0:T(8,128)}), (f32[256,768]{1,0:T(8,128)}, f32[256,256]{1,0:T(8,128)}, f32[256,1024]{1,0:T(8,128)}, ...) | async-done | bytes 3145744 | tf_op jit(solution)/shard_map/psum | solution.py:232
  (140 shorter events, 38.1 us)
Async XLA Ops:
  7.2 141.5 %copy-start = (bf16[256,1024]{1,0:T(8,128)(2,1)S(1)}, bf16[256,1024]{1,0:T(8,128)(2,1)}, u32[]{:S(2)}) copy-start(bf16[256,1024]{1,0:T(8,128)(2,1)} %param.24) | copy-start | bytes 1572868
  7.2 58.4 %reduce-scatter.11.cloned.1.call-start = ((), (), s32[]{:S(2)}) async-start(), calls=%async_computation.10 | async-start | bytes 1966080 | tf_op jit(solution)/shard_map/reduce_scatter | solution.py:73
  22.7 9.1 %copy-start.25 = (f32[512]{0:T(512)S(1)}, f32[512]{0:T(512)}, u32[]{:S(2)}) copy-start(f32[512]{0:T(512)} %param.19) | copy-start | bytes 6148
  31.8 97.5 %reduce-scatter.13.cloned.1.call-start = ((), (), s32[]{:S(2)}) async-start(), calls=%async_computation.11 | async-start | bytes 655360 | tf_op jit(solution)/shard_map/reduce_scatter | solution.py:84
  80.2 27.8 %copy-start.18 = (bf16[256,256]{1,0:T(8,128)(2,1)S(1)}, bf16[256,256]{1,0:T(8,128)(2,1)}, u32[]{:S(2)}) copy-start(bf16[256,256]{1,0:T(8,128)(2,1)} %param.20) | copy-start | bytes 393220
  94.2 15.0 %copy-start.21 = (bf16[128,256]{1,0:T(8,128)(2,1)S(1)}, bf16[128,256]{1,0:T(8,128)(2,1)}, u32[]{:S(2)}) copy-start(bf16[128,256]{1,0:T(8,128)(2,1)} %param.15) | copy-start | bytes 196612
  94.2 21.5 %copy-start.12 = (bf16[1024,256]{1,0:T(8,128)(2,1)S(1)}, bf16[1024,256]{1,0:T(8,128)(2,1)}, u32[]{:S(2)}) copy-start(bf16[1024,256]{1,0:T(8,128)(2,1)} %param.26) | copy-start | bytes 1572868
  109.1 66.1 %reduce-scatter.19.cloned.1.call-start = ((), (), s32[]{:S(2)}) async-start(), calls=%async_computation.15 | async-start | bytes 2621440 | tf_op jit(solution)/shard_map/reduce_scatter | solution.py:73
  115.6 13.6 %copy-start.13 = (bf16[128,256]{1,0:T(8,128)(2,1)S(1)}, bf16[128,256]{1,0:T(8,128)(2,1)}, u32[]{:S(2)}) copy-start(bf16[128,256]{1,0:T(8,128)(2,1)} %param.14) | copy-start | bytes 196612
  115.6 13.6 %copy-start.26 = (f32[256]{0:T(256)S(1)}, f32[256]{0:T(256)}, u32[]{:S(2)}) copy-start(f32[256]{0:T(256)} %param.21) | copy-start | bytes 3076
  115.6 26.4 %copy-start.22 = (f32[256]{0:T(256)S(1)}, f32[256]{0:T(256)}, u32[]{:S(2)}) copy-start(f32[256]{0:T(256)} %param.22) | copy-start | bytes 3076
  115.6 26.4 %copy-start.27 = (f32[256]{0:T(256)S(1)}, f32[256]{0:T(256)}, u32[]{:S(2)}) copy-start(f32[256]{0:T(256)} %param.23) | copy-start | bytes 3076
  117.5 102.6 %reduce-scatter.15.cloned.1.call-start = ((), (), s32[]{:S(2)}) async-start(), calls=%async_computation.12 | async-start | bytes 2621440 | tf_op jit(solution)/shard_map/reduce_scatter | solution.py:73
  148.7 71.5 %copy-start.24 = (f32[1024]{0:T(1024)S(1)}, f32[1024]{0:T(1024)}, u32[]{:S(2)}) copy-start(f32[1024]{0:T(1024)} %param.25) | copy-start | bytes 12292
  150.4 99.5 %all-gather.5.cloned.1.call-start = ((), (), s32[]{:S(2)}) async-start(), calls=%async_computation.16 | async-start | bytes 1310720 | tf_op jit(solution)/shard_map/all_gather | solution.py:64
  222.5 56.7 %all-gather.3.cloned.1.call-start = ((), (), s32[]{:S(2)}) async-start(), calls=%async_computation.13 | async-start | bytes 1310720 | tf_op jit(solution)/shard_map/all_gather | solution.py:64
  223.1 80.2 %reduce-scatter.21.cloned.1.call-start = ((), (), s32[]{:S(2)}) async-start(), calls=%async_computation.17 | async-start | bytes 655360 | tf_op jit(solution)/shard_map/reduce_scatter | solution.py:84
  252.4 75.7 %copy-start.28 = (f32[256]{0:T(256)S(1)}, f32[256]{0:T(256)}, u32[]{:S(2)}) copy-start(f32[256]{0:T(256)} %param.27) | copy-start | bytes 3076
  252.4 75.7 %reduce-scatter.17.cloned.1.call-start = ((), (), s32[]{:S(2)}) async-start(), calls=%async_computation.14 | async-start | bytes 655360 | tf_op jit(solution)/shard_map/reduce_scatter | solution.py:84
  281.8 77.6 %reduce-scatter.23.cloned.1.call-start = ((), (), s32[]{:S(2)}) async-start(), calls=%async_computation.18 | async-start | bytes 655360 | tf_op jit(solution)/shard_map/reduce_scatter | solution.py:73
  329.8 31.8 %copy-start.14 = (f32[128,256]{1,0:T(8,128)}, f32[128,256]{1,0:T(8,128)S(1)}, u32[]{:S(2)}) copy-start(f32[128,256]{1,0:T(8,128)S(1)} %get-tuple-element.109) | copy-start | bytes 393220
  337.3 44.7 %reduce-scatter.27.cloned.1.call-start = ((), (), s32[]{:S(2)}) async-start(), calls=%async_computation.20 | async-start | bytes 655360 | tf_op jit(solution)/shard_map/reduce_scatter | solution.py:219
  361.5 43.4 %reduce-scatter.25.cloned.1.call-start = ((), (), s32[]{:S(2)}) async-start(), calls=%async_computation.19 | async-start | bytes 655360 | tf_op jit(solution)/shard_map/reduce_scatter | solution.py:218
  363.1 89.2 %reduce-scatter.29.cloned.1.call-start = ((), (), s32[]{:S(2)}) async-start(), calls=%async_computation.21 | async-start | bytes 655360 | tf_op jit(solution)/shard_map/reduce_scatter | solution.py:84
  383.0 42.3 %copy-start.1 = (bf16[512,1024]{1,0:T(8,128)(2,1)S(1)}, bf16[512,1024]{1,0:T(8,128)(2,1)}, u32[]{:S(2)}) copy-start(bf16[512,1024]{1,0:T(8,128)(2,1)} %all-gather.5.cloned.1.call-done) | copy-start | bytes 3145732
  422.9 4.9 copy-start.2
  425.3 110.7 %all-reduce.9.cloned.1.call-start = ((), (), s32[]{:S(2)}) async-start(), calls=%async_computation.22 | async-start | bytes 6291456 | tf_op jit(solution)/shard_map/psum | solution.py:232
  425.3 3.9 copy-start.6
  425.3 3.9 copy-start.8
  431.5 20.9 %copy-start.23 = (f32[256]{0:T(256)S(1)}, f32[256]{0:T(256)}, u32[]{:S(2)}) copy-start(f32[256]{0:T(256)} %param.16) | copy-start | bytes 3076
  431.5 43.3 %copy-start.15 = (f32[128,256]{1,0:T(8,128)S(1)}, f32[128,256]{1,0:T(8,128)}, u32[]{:S(2)}) copy-start(f32[128,256]{1,0:T(8,128)} %copy-done.14) | copy-start | bytes 393220
  536.0 4.9 copy-start.16
  (10 other events, 15.0 us)
Sparse Core Ops, SparseCore 0:
  31.9 33.6 reduce-scatter.10
  109.2 19.9 reduce-scatter.12
  131.5 43.6 reduce-scatter.18
  177.4 42.6 reduce-scatter.14
  222.7 27.1 all-gather.4
  251.9 27.3 all-gather.2
  282.3 20.9 reduce-scatter.20
  306.4 21.6 reduce-scatter.16
  337.5 21.8 reduce-scatter.22
  362.0 20.0 reduce-scatter.26
  384.9 20.0 reduce-scatter.24
  425.4 20.7 reduce-scatter.28
  449.8 86.1 all-reduce.8
where the time goes:
time: 549 us; the launch traced here: 548 us
  waiting for transfers between devices  324 us (59%)
  blocking collectives  158 us (29%)
  matrix products  26.1 us (5%)
  other arithmetic  14.3 us (3%)
  between operations  14.2 us (3%)
  local copies, waits for them, and re-layouts  11 us (2%)
    reduce_scatter x4, waiting for transfers between devices, to_cols(): lax.psum_scatter(term(jnp.int32(0), lax.axis_size('col') * own_rows), 'co...  125 us
    psum x1, waiting for transfers between devices, local(): lax.psum((grad_qkv, grad_out, grad_up, grad_down), 'dp')  59.5 us
    all_gather x2, waiting for transfers between devices, cols_in(): return lax.all_gather(block, 'col', axis=0, tiled=True)  53.5 us
    psum x4, blocking collectives, feature_stats(): return lax.psum((first_part, second_part), 'col')  45.4 us
    reduce_scatter x4, waiting for transfers between devices, to_rows(): lax.psum_scatter(term(jnp.int32(0), lax.axis_size('row') * own_rows), 'ro...  45.2 us
    all_gather x2, blocking collectives, cols_in(): return lax.all_gather(block, 'col', axis=0, tiled=True)  29.8 us
    all_gather x4, blocking collectives, rows_in(): return lax.all_gather(block, 'row', axis=0, tiled=True)  23.1 us
    reduce_scatter x1, waiting for transfers between devices, local(): lax.psum_scatter(key_acc.reshape(group_rows, -1), 'col', scatter_dimensio...  22 us
  transfers between devices with their start and end apart: 13, of which 12 were waited for; matrix products, arithmetic and copies ran while one was open for 4% of the time, Pallas kernels for 0%

commit v1 on v0

--- a/solution.py
+++ b/solution.py
@@ -9,6 +9,19 @@
 EPS = 1e-05
 GELU_C = 0.7978845608028654
 GELU_A = 0.044715
+
+
+def collect(x, axis, dim):
+    peers, index, span = (lax.axis_size(axis), lax.axis_index(axis), x.shape[dim])
+    forward = [(i, (i + 1) % peers) for i in range(peers)]
+    out = jnp.zeros((*x.shape[:dim], peers * span, *x.shape[dim + 1 :]), x.dtype)
+    carried = x
+    for step in range(peers):
+        owner = (index - step) % peers
+        out = lax.dynamic_update_slice_in_dim(out, carried, owner * span, axis=dim)
+        if step < peers - 1:
+            carried = lax.ppermute(carried, axis, forward)
+    return out
 
 
 def gelu_pair(hidden):
@@ -61,7 +74,7 @@
 
 
 def cols_in(block):
-    return lax.all_gather(block, "col", axis=0, tiled=True)
+    return collect(block, "col", 0)
 
 
 def to_cols(whole, matrix, transposed):

time: 549 us -> 529 us (0.964)
  blocking collectives: 158 us -> 127 us
    ppermute x0 -> x12, waiting for transfers between devices: none -> 83.4 us  [collect(): carried = lax.ppermute(carried, axis, forward)]
    all_gather x2 -> x0, waiting for transfers between devices: 53.5 us -> none  [cols_in(): return lax.all_gather(block, 'col', axis=0, tiled=True)]
    all_gather x2 -> x0, blocking collectives: 29.8 us -> none  [cols_in(): return lax.all_gather(block, 'col', axis=0, tiled=True)]
    reduce_scatter x4, waiting for transfers between devices: 45.2 us -> 22.7 us  [to_rows(): lax.psum_scatter(term(jnp.int32(0), lax.axis_size('row') * own_rows), 'ro...]
  transfers between devices with their start and end apart: 13 -> 23, of which waited for: 12 -> 21; matrix products, arithmetic and copies ran while one was open for 4% -> 6% of each run, Pallas kernels for 0% -> 0%
where the time goes in v1:
time: 529 us; the launch traced here: 528 us
  waiting for transfers between devices  328 us (62%)
  blocking collectives  127 us (24%)
  matrix products  27.9 us (5%)
  other arithmetic  15.6 us (3%)
  between operations  14.5 us (3%)
  local copies, waits for them, and re-layouts  13.9 us (3%)
    reduce_scatter x4, waiting for transfers between devices, to_cols(): lax.psum_scatter(term(jnp.int32(0), lax.axis_size('col') * own_rows), 'co...  124 us
    ppermute x12, waiting for transfers between devices, collect(): carried = lax.ppermute(carried, axis, forward)  83.4 us
    psum x1, waiting for transfers between devices, local(): lax.psum((grad_qkv, grad_out, grad_up, grad_down), 'dp')  58.9 us
    psum x4, blocking collectives, feature_stats(): return lax.psum((first_part, second_part), 'col')  45.5 us
    all_gather x4, blocking collectives, rows_in(): return lax.all_gather(block, 'row', axis=0, tiled=True)  23.6 us
    reduce_scatter x4, waiting for transfers between devices, to_rows(): lax.psum_scatter(term(jnp.int32(0), lax.axis_size('row') * own_rows), 'ro...  22.7 us
    reduce_scatter x1, waiting for transfers between devices, local(): lax.psum_scatter(key_acc.reshape(group_rows, -1), 'col', scatter_dimensio...  22.1 us
    psum x1, blocking collectives, local(): lax.psum((qv_bias_part, up_bias_part), ('dp', 'col'))  18.5 us
  transfers between devices with their start and end apart: 23, of which 21 were waited for; matrix products, arithmetic and copies ran while one was open for 6% of the time, Pallas kernels for 0%

profile of v1, /device:TPU:0, one launch (start us, length us, event | category | flops | bytes accessed | tf_op | source)
XLA Modules:
  0.0 527.8 jit_solution(15325113428389233594)
XLA Ops:
  8.2 13.5 %all-reduce.5 = (f32[128]{0:T(128)S(1)}, f32[128]{0:T(128)S(1)}) all-reduce(f32[128]{0:T(128)S(1)} %get-tuple-element.85, f32[128]{0:T(128)S(1)} %get-tuple-element.84), channel_id=1, replica_groups=mesh['dp'=2,'row'=4,'col'=4] {'col'}, use_global_device_ids=true, to_apply=%region_3.0 | all-reduce | flops 256 | bytes 2048 | tf_op jit(solution)/shard_map/psum | solution.py:38
  22.7 5.8 %all_gather.18 = bf16[512,256]{1,0:T(8,128)(2,1)S(1)} all-gather(bf16[128,256]{1,0:T(8,128)(2,1)S(1)} %fusion.26), channel_id=1, replica_groups=mesh['dp'=2,'row'=4,'col'=4] {'row'}, dimensions={0}, use_global_device_ids=true | all-gather | bytes 327680 | tf_op jit(solution)/shard_map/all_gather | solution.py:73
  32.4 33.2 %reduce-scatter.11.cloned.1.call-done = f32[128,768]{1,0:T(8,128)} async-done(((f32[512,768]{1,0:T(8,128)}), f32[128,768]{1,0:T(8,128)}) %reduce-scatter.11.cloned.1.call-update) | async-done | bytes 393232 | tf_op jit(solution)/shard_map/reduce_scatter | solution.py:86
  66.9 13.4 %all_gather.19 = bf16[512,256]{0,1:T(8,128)(2,1)S(1)} all-gather(bf16[128,256]{0,1:T(8,128)(2,1)S(1)} %fusion.36), channel_id=1, replica_groups=mesh['dp'=2,'row'=4,'col'=4] {'col'}, dimensions={0}, use_global_device_ids=true | all-gather | bytes 327680 | tf_op jit(solution)/shard_map/all_gather | solution.py:149
  80.2 13.1 %all_gather.20 = bf16[512,256]{0,1:T(8,128)(2,1)S(1)} all-gather(bf16[128,256]{0,1:T(8,128)(2,1)S(1)} %bitcast.93), channel_id=1, replica_groups=mesh['dp'=2,'row'=4,'col'=4] {'col'}, dimensions={0}, use_global_device_ids=true | all-gather | bytes 327680 | tf_op jit(solution)/shard_map/all_gather | solution.py:148
  95.2 6.0 %collective-permute-done = bf16[128,256]{0,1:T(8,128)(2,1)S(1)} collective-permute-done((bf16[128,256]{0,1:T(8,128)(2,1)S(1)}, bf16[128,256]{0,1:T(8,128)(2,1)S(1)}, u32[]{:S(2)}, u32[]{:S(2)}) %collective-permute-start) | collective-permute-done | bytes 65568 | tf_op jit(solution)/shard_map/ppermute | solution.py:23
  101.2 6.0 %collective-permute-done.1 = bf16[128,256]{0,1:T(8,128)(2,1)S(1)} collective-permute-done((bf16[128,256]{0,1:T(8,128)(2,1)S(1)}, bf16[128,256]{0,1:T(8,128)(2,1)S(1)}, u32[]{:S(2)}, u32[]{:S(2)}) %collective-permute-start.1) | collective-permute-done | bytes 65568 | tf_op jit(solution)/shard_map/ppermute | solution.py:23
  107.3 6.0 %collective-permute-done.2 = bf16[128,256]{0,1:T(8,128)(2,1)S(1)} collective-permute-done((bf16[128,256]{0,1:T(8,128)(2,1)S(1)}, bf16[128,256]{0,1:T(8,128)(2,1)S(1)}, u32[]{:S(2)}, u32[]{:S(2)}) %collective-permute-start.2) | collective-permute-done | bytes 65568 | tf_op jit(solution)/shard_map/ppermute | solution.py:23
  115.2 5.8 %all_gather.22 = bf16[512,256]{1,0:T(8,128)(2,1)S(1)} all-gather(bf16[128,256]{1,0:T(8,128)(2,1)S(1)} %copy-done.24), channel_id=1, replica_groups=mesh['dp'=2,'row'=4,'col'=4] {'row'}, dimensions={0}, use_global_device_ids=true | all-gather | bytes 327680 | tf_op jit(solution)/shard_map/all_gather | solution.py:73
  123.6 11.4 %reduce-scatter.13.cloned.1.call-done = f32[128,256]{1,0:T(8,128)} async-done(((f32[512,256]{1,0:T(8,128)}), f32[128,256]{1,0:T(8,128)}) %reduce-scatter.13.cloned.1.call-update) | async-done | bytes 131088 | tf_op jit(solution)/shard_map/reduce_scatter | solution.py:97
  136.0 11.8 %all-reduce.4 = (f32[128]{0:T(128)S(1)}, f32[128]{0:T(128)S(1)}) all-reduce(f32[128]{0:T(128)S(1)} %get-tuple-element.83, f32[128]{0:T(128)S(1)} %get-tuple-element.82), channel_id=1, replica_groups=mesh['dp'=2,'row'=4,'col'=4] {'col'}, use_global_device_ids=true, to_apply=%region_10.11 | all-reduce | flops 256 | bytes 2048 | tf_op jit(solution)/shard_map/psum | solution.py:38
  147.9 6.2 %all_gather.21 = bf16[512,256]{1,0:T(8,128)(2,1)} all-gather(bf16[128,256]{1,0:T(8,128)(2,1)S(1)} %add_convert_fusion.1), channel_id=1, replica_groups=mesh['dp'=2,'row'=4,'col'=4] {'row'}, dimensions={0}, use_global_device_ids=true | all-gather | bytes 327680 | tf_op jit(solution)/shard_map/all_gather | solution.py:73
  156.9 24.0 %reduce-scatter.19.cloned.1.call-done = f32[128,1024]{1,0:T(8,128)} async-done(((f32[512,1024]{1,0:T(8,128)}), f32[128,1024]{1,0:T(8,128)}) %reduce-scatter.19.cloned.1.call-update) | async-done | bytes 524304 | tf_op jit(solution)/shard_map/reduce_scatter | solution.py:86
  180.9 44.9 %reduce-scatter.15.cloned.1.call-done = f32[128,1024]{1,0:T(8,128)} async-done(((f32[512,1024]{1,0:T(8,128)}), f32[128,1024]{1,0:T(8,128)}) %reduce-scatter.15.cloned.1.call-update) | async-done | bytes 524304 | tf_op jit(solution)/shard_map/reduce_scatter | solution.py:86
  228.4 8.8 %collective-permute-done.6 = bf16[128,1024]{1,0:T(8,128)(2,1)S(1)} collective-permute-done((bf16[128,1024]{1,0:T(8,128)(2,1)S(1)}, bf16[128,1024]{1,0:T(8,128)(2,1)S(1)}, u32[]{:S(2)}, u32[]{:S(2)}) %collective-permute-start.6) | collective-permute-done | bytes 262176 | tf_op jit(solution)/shard_map/ppermute | solution.py:23
  237.2 8.6 %collective-permute-done.7 = bf16[128,1024]{1,0:T(8,128)(2,1)S(1)} collective-permute-done((bf16[128,1024]{1,0:T(8,128)(2,1)S(1)}, bf16[128,1024]{1,0:T(8,128)(2,1)S(1)}, u32[]{:S(2)}, u32[]{:S(2)}) %collective-permute-start.7) | collective-permute-done | bytes 262176 | tf_op jit(solution)/shard_map/ppermute | solution.py:23
  246.9 9.5 %collective-permute-done.8 = bf16[128,1024]{1,0:T(8,128)(2,1)S(1)} collective-permute-done((bf16[128,1024]{1,0:T(8,128)(2,1)S(1)}, bf16[128,1024]{1,0:T(8,128)(2,1)S(1)}, u32[]{:S(2)}, u32[]{:S(2)}) %collective-permute-start.8) | collective-permute-done | bytes 262176 | tf_op jit(solution)/shard_map/ppermute | solution.py:23
  259.2 8.2 %collective-permute-done.4 = bf16[128,1024]{1,0:T(8,128)(2,1)S(1)} collective-permute-done((bf16[128,1024]{1,0:T(8,128)(2,1)S(1)}, bf16[128,1024]{1,0:T(8,128)(2,1)S(1)}, u32[]{:S(2)}, u32[]{:S(2)}) %collective-permute-start.4) | collective-permute-done | bytes 262176 | tf_op jit(solution)/shard_map/ppermute | solution.py:23
  268.8 6.7 %collective-permute-done.5 = bf16[128,1024]{1,0:T(8,128)(2,1)S(1)} collective-permute-done((bf16[128,1024]{1,0:T(8,128)(2,1)S(1)}, bf16[128,1024]{1,0:T(8,128)(2,1)S(1)}, u32[]{:S(2)}, u32[]{:S(2)}) %collective-permute-start.5) | collective-permute-done | bytes 262176 | tf_op jit(solution)/shard_map/ppermute | solution.py:23
  280.6 10.3 %all-reduce.3 = (f32[128]{0:T(128)S(1)}, f32[128]{0:T(128)S(1)}) all-reduce(f32[128]{0:T(128)S(1)} %get-tuple-element.63, f32[128]{0:T(128)S(1)} %get-tuple-element.67), channel_id=1, replica_groups=mesh['dp'=2,'row'=4,'col'=4] {'col'}, use_global_device_ids=true, to_apply=%region_18.19 | all-reduce | flops 256 | bytes 2048 | tf_op jit(solution)/shard_map/psum | solution.py:38
  290.9 11.3 %reduce-scatter.17.cloned.1.call-done = f32[128,256]{1,0:T(8,128)} async-done(((f32[512,256]{1,0:T(8,128)}), f32[128,256]{1,0:T(8,128)}) %reduce-scatter.17.cloned.1.call-update) | async-done | bytes 131088 | tf_op jit(solution)/shard_map/reduce_scatter | solution.py:97
  304.4 5.8 %all_gather.23 = bf16[512,256]{1,0:T(8,128)(2,1)S(1)} all-gather(bf16[128,256]{1,0:T(8,128)(2,1)S(1)} %convert_element_type.98), channel_id=1, replica_groups=mesh['dp'=2,'row'=4,'col'=4] {'row'}, dimensions={0}, use_global_device_ids=true | all-gather | bytes 327680 | tf_op jit(solution)/shard_map/all_gather | solution.py:73
  312.0 21.9 %reduce-scatter.23.cloned.1.call-done = f32[128,256]{1,0:T(8,128)} async-done(((f32[512,256]{1,0:T(8,128)}), f32[128,256]{1,0:T(8,128)}) %reduce-scatter.23.cloned.1.call-update) | async-done | bytes 131088 | tf_op jit(solution)/shard_map/reduce_scatter | solution.py:86
  340.6 16.3 %reduce-scatter.27.cloned.1.call-done = f32[128,256]{0,1:T(8,128)} async-done(((f32[512,256]{0,1:T(8,128)}), f32[128,256]{0,1:T(8,128)}) %reduce-scatter.27.cloned.1.call-update) | async-done | bytes 131088 | tf_op jit(solution)/shard_map/reduce_scatter | solution.py:232
  357.8 22.1 %reduce-scatter.25.cloned.1.call-done = f32[128,256]{0,1:T(8,128)} async-done(((f32[512,256]{0,1:T(8,128)}), f32[128,256]{0,1:T(8,128)}) %reduce-scatter.25.cloned.1.call-update) | async-done | bytes 131088 | tf_op jit(solution)/shard_map/reduce_scatter | solution.py:231
  380.9 7.5 %collective-permute-done.9 = bf16[128,768]{0,1:T(8,128)(2,1)S(1)} collective-permute-done((bf16[128,768]{0,1:T(8,128)(2,1)S(1)}, bf16[128,768]{0,1:T(8,128)(2,1)S(1)}, u32[]{:S(2)}, u32[]{:S(2)}) %collective-permute-start.9) | collective-permute-done | bytes 196640 | tf_op jit(solution)/shard_map/ppermute | solution.py:23
  388.5 7.3 %collective-permute-done.10 = bf16[128,768]{0,1:T(8,128)(2,1)S(1)} collective-permute-done((bf16[128,768]{0,1:T(8,128)(2,1)S(1)}, bf16[128,768]{0,1:T(8,128)(2,1)S(1)}, u32[]{:S(2)}, u32[]{:S(2)}) %collective-permute-start.10) | collective-permute-done | bytes 196640 | tf_op jit(solution)/shard_map/ppermute | solution.py:23
  396.0 7.4 %collective-permute-done.11 = bf16[128,768]{0,1:T(8,128)(2,1)S(1)} collective-permute-done((bf16[128,768]{0,1:T(8,128)(2,1)S(1)}, bf16[128,768]{0,1:T(8,128)(2,1)S(1)}, u32[]{:S(2)}, u32[]{:S(2)}) %collective-permute-start.11) | collective-permute-done | bytes 196640 | tf_op jit(solution)/shard_map/ppermute | solution.py:23
  412.3 18.5 %all-reduce = (f32[512]{0:T(512)}, f32[1024]{0:T(1024)}) all-reduce(f32[512]{0:T(512)S(1)} %reshape.258, f32[1024]{0:T(1024)S(1)} %get-tuple-element.106), channel_id=1, replica_groups=mesh['dp'=2,'row'=4,'col'=4] {'dp','col'}, use_global_device_ids=true, to_apply=%region_34.35 | all-reduce | flops 1536 | bytes 12288 | tf_op jit(solution)/shard_map/psum | solution.py:259
  431.8 9.9 %all-reduce.2 = (f32[128]{0:T(128)S(1)}, f32[128]{0:T(128)S(1)}) all-reduce(f32[128]{0:T(128)S(1)} %get-tuple-element.65, f32[128]{0:T(128)S(1)} %get-tuple-element.66), channel_id=1, replica_groups=mesh['dp'=2,'row'=4,'col'=4] {'col'}, use_global_device_ids=true, to_apply=%region_27.28 | all-reduce | flops 256 | bytes 2048 | tf_op jit(solution)/shard_map/psum | solution.py:38
  441.8 13.0 %all-reduce.1 = (f32[256]{0:T(256)}, f32[256]{0:T(256)}, f32[256]{0:T(256)}, f32[256]{0:T(256)}, f32[256]{0:T(256)}, /*index=5*/f32[256]{0:T(256)}) all-reduce(f32[256]{0:T(256)S(1)} %get-tuple-element.64, f32[256]{0:T(256)S(1)} %get-tuple-element.81, f32[256]{0:T(256)S(1)} %copy-done.31, ...), channel_id=1, replica_groups=mesh['dp'=2,'row'=4,'col'=4] {'dp','row'}, use_global_device_ids=true, to_apply=%region_29.30 | all-reduce | flops 1536 | bytes 12288 | tf_op jit(solution)/shard_map/psum | solution.py:248
  456.5 58.9 %all-reduce.9.cloned.1.call-done = (f32[256,768]{1,0:T(8,128)}, f32[256,256]{1,0:T(8,128)}, f32[256,1024]{1,0:T(8,128)}, f32[1024,256]{1,0:T(8,128)}) async-done(((f32[256,768]{1,0:T(8,128)}, f32[256,256]{1,0:T(8,128)}, f32[256,1024]{1,0:T(8,128)}, f32[1024,256]{1,0:T(8,128)}), (f32[256,768]{1,0:T(8,128)}, f32[256,256]{1,0:T(8,128)}, f32[256,1024]{1,0:T(8,128)}, ...) | async-done | bytes 3145744 | tf_op jit(solution)/shard_map/psum | solution.py:245
  (192 shorter events, 60.3 us)
Async XLA Ops:
  7.2 147.0 %copy-start = (bf16[256,1024]{1,0:T(8,128)(2,1)S(1)}, bf16[256,1024]{1,0:T(8,128)(2,1)}, u32[]{:S(2)}) copy-start(bf16[256,1024]{1,0:T(8,128)(2,1)} %param.24) | copy-start | bytes 1572868
  7.2 58.3 %reduce-scatter.11.cloned.1.call-start = ((), (), s32[]{:S(2)}) async-start(), calls=%async_computation.10 | async-start | bytes 1966080 | tf_op jit(solution)/shard_map/reduce_scatter | solution.py:86
  31.7 103.2 %reduce-scatter.13.cloned.1.call-start = ((), (), s32[]{:S(2)}) async-start(), calls=%async_computation.11 | async-start | bytes 655360 | tf_op jit(solution)/shard_map/reduce_scatter | solution.py:97
  32.0 62.7 %copy-start.28 = (f32[4,1,64]{2,1,0:T(1,128)}, f32[4,1,64]{2,1,0:T(1,128)S(1)}, u32[]{:S(2)}) copy-start(f32[4,1,64]{2,1,0:T(1,128)S(1)} %get-tuple-element.117) | copy-start | bytes 3076
  95.1 6.1 %collective-permute-start = (bf16[128,256]{0,1:T(8,128)(2,1)S(1)}, bf16[128,256]{0,1:T(8,128)(2,1)S(1)}, u32[]{:S(2)}, u32[]{:S(2)}) collective-permute-start(bf16[128,256]{0,1:T(8,128)(2,1)S(1)} %bitcast.90), channel_id=1, source_target_pairs={{0,1},{1,2},{2,3},{3,0},{4,5},{5,6},{6,7},{7,4},{8,9},{9,10},{10,1... | collective-permute-start | bytes 196616 | tf_op jit(solution)/shard_map/ppermute | solution.py:23
  101.2 6.1 %collective-permute-start.1 = (bf16[128,256]{0,1:T(8,128)(2,1)S(1)}, bf16[128,256]{0,1:T(8,128)(2,1)S(1)}, u32[]{:S(2)}, u32[]{:S(2)}) collective-permute-start(bf16[128,256]{0,1:T(8,128)(2,1)S(1)} %collective-permute-done), channel_id=1, source_target_pairs={{0,1},{1,2},{2,3},{3,0},{4,5},{5,6},{6,7},{7,4},{8,9},{9,10},{10,1... | collective-permute-start | bytes 196616 | tf_op jit(solution)/shard_map/ppermute | solution.py:23
  107.2 6.1 %collective-permute-start.2 = (bf16[128,256]{0,1:T(8,128)(2,1)S(1)}, bf16[128,256]{0,1:T(8,128)(2,1)S(1)}, u32[]{:S(2)}, u32[]{:S(2)}) collective-permute-start(bf16[128,256]{0,1:T(8,128)(2,1)S(1)} %collective-permute-done.1), channel_id=1, source_target_pairs={{0,1},{1,2},{2,3},{3,0},{4,5},{5,6},{6,7},{7,4},{8,9},{9,10},{10,1... | collective-permute-start | bytes 196616 | tf_op jit(solution)/shard_map/ppermute | solution.py:23
  115.1 65.8 %reduce-scatter.19.cloned.1.call-start = ((), (), s32[]{:S(2)}) async-start(), calls=%async_computation.14 | async-start | bytes 2621440 | tf_op jit(solution)/shard_map/reduce_scatter | solution.py:86
  123.5 102.3 %reduce-scatter.15.cloned.1.call-start = ((), (), s32[]{:S(2)}) async-start(), calls=%async_computation.12 | async-start | bytes 2621440 | tf_op jit(solution)/shard_map/reduce_scatter | solution.py:86
  154.1 71.7 %copy-start.25 = (f32[1024]{0:T(1024)S(1)}, f32[1024]{0:T(1024)}, u32[]{:S(2)}) copy-start(f32[1024]{0:T(1024)} %param.25) | copy-start | bytes 12292
  156.9 122.1 %reduce-scatter.21.cloned.1.call-start = ((), (), s32[]{:S(2)}) async-start(), calls=%async_computation.15 | async-start | bytes 655360 | tf_op jit(solution)/shard_map/reduce_scatter | solution.py:97
  227.7 9.5 %collective-permute-start.6 = (bf16[128,1024]{1,0:T(8,128)(2,1)S(1)}, bf16[128,1024]{1,0:T(8,128)(2,1)S(1)}, u32[]{:S(2)}, u32[]{:S(2)}) collective-permute-start(bf16[128,1024]{1,0:T(8,128)(2,1)S(1)} %get-tuple-element.111), channel_id=1, source_target_pairs={{0,1},{1,2},{2,3},{3,0},{4,5},{5,6},{6,7},{7,4},{8,9},{9,10},{10,1... | collective-permute-start | bytes 786440 | tf_op jit(solution)/shard_map/ppermute | solution.py:23
  237.2 8.6 %collective-permute-start.7 = (bf16[128,1024]{1,0:T(8,128)(2,1)S(1)}, bf16[128,1024]{1,0:T(8,128)(2,1)S(1)}, u32[]{:S(2)}, u32[]{:S(2)}) collective-permute-start(bf16[128,1024]{1,0:T(8,128)(2,1)S(1)} %collective-permute-done.6), channel_id=1, source_target_pairs={{0,1},{1,2},{2,3},{3,0},{4,5},{5,6},{6,7},{7,4},{8,9},{9,10},{10,1... | collective-permute-start | bytes 786440 | tf_op jit(solution)/shard_map/ppermute | solution.py:23
  245.8 10.6 %collective-permute-start.8 = (bf16[128,1024]{1,0:T(8,128)(2,1)S(1)}, bf16[128,1024]{1,0:T(8,128)(2,1)S(1)}, u32[]{:S(2)}, u32[]{:S(2)}) collective-permute-start(bf16[128,1024]{1,0:T(8,128)(2,1)S(1)} %collective-permute-done.7), channel_id=1, source_target_pairs={{0,1},{1,2},{2,3},{3,0},{4,5},{5,6},{6,7},{7,4},{8,9},{9,10},{10,1... | collective-permute-start | bytes 786440 | tf_op jit(solution)/shard_map/ppermute | solution.py:23
  246.8 12.3 %collective-permute-start.3 = (bf16[128,1024]{1,0:T(8,128)(2,1)}, bf16[128,1024]{1,0:T(8,128)(2,1)S(1)}, u32[]{:S(2)}, u32[]{:S(2)}) collective-permute-start(bf16[128,1024]{1,0:T(8,128)(2,1)} %get-tuple-element.113), channel_id=1, source_target_pairs={{0,1},{1,2},{2,3},{3,0},{4,5},{5,6},{6,7},{7,4},{8,9},{9,10},{10,1... | collective-permute-start | bytes 786440 | tf_op jit(solution)/shard_map/ppermute | solution.py:23
  257.7 44.5 %reduce-scatter.17.cloned.1.call-start = ((), (), s32[]{:S(2)}) async-start(), calls=%async_computation.13 | async-start | bytes 655360 | tf_op jit(solution)/shard_map/reduce_scatter | solution.py:97
  259.1 8.2 %collective-permute-start.4 = (bf16[128,1024]{1,0:T(8,128)(2,1)S(1)}, bf16[128,1024]{1,0:T(8,128)(2,1)S(1)}, u32[]{:S(2)}, u32[]{:S(2)}) collective-permute-start(bf16[128,1024]{1,0:T(8,128)(2,1)S(1)} %collective-permute-done.3), channel_id=1, source_target_pairs={{0,1},{1,2},{2,3},{3,0},{4,5},{5,6},{6,7},{7,4},{8,9},{9,10},{10,1... | collective-permute-start | bytes 786440 | tf_op jit(solution)/shard_map/ppermute | solution.py:23
  267.3 8.2 %collective-permute-start.5 = (bf16[128,1024]{1,0:T(8,128)(2,1)S(1)}, bf16[128,1024]{1,0:T(8,128)(2,1)S(1)}, u32[]{:S(2)}, u32[]{:S(2)}) collective-permute-start(bf16[128,1024]{1,0:T(8,128)(2,1)S(1)} %collective-permute-done.4), channel_id=1, source_target_pairs={{0,1},{1,2},{2,3},{3,0},{4,5},{5,6},{6,7},{7,4},{8,9},{9,10},{10,1... | collective-permute-start | bytes 786440 | tf_op jit(solution)/shard_map/ppermute | solution.py:23
  268.0 34.1 %copy-start.36 = (f32[256]{0:T(256)S(1)}, f32[256]{0:T(256)}, u32[]{:S(2)}) copy-start(f32[256]{0:T(256)} %param.27) | copy-start | bytes 3076
  276.2 34.6 %copy-start.21 = (bf16[256,256]{1,0:T(8,128)(2,1)S(1)}, bf16[256,256]{1,0:T(8,128)(2,1)}, u32[]{:S(2)}) copy-start(bf16[256,256]{1,0:T(8,128)(2,1)} %param.20) | copy-start | bytes 393220
  278.9 55.0 %reduce-scatter.23.cloned.1.call-start = ((), (), s32[]{:S(2)}) async-start(), calls=%async_computation.16 | async-start | bytes 655360 | tf_op jit(solution)/shard_map/reduce_scatter | solution.py:86
  304.4 31.8 %copy-start.15 = (f32[128,256]{1,0:T(8,128)}, f32[128,256]{1,0:T(8,128)S(1)}, u32[]{:S(2)}) copy-start(f32[128,256]{1,0:T(8,128)S(1)} %get-tuple-element.109) | copy-start | bytes 393220
  311.9 45.0 %reduce-scatter.27.cloned.1.call-start = ((), (), s32[]{:S(2)}) async-start(), calls=%async_computation.18 | async-start | bytes 655360 | tf_op jit(solution)/shard_map/reduce_scatter | solution.py:232
  336.2 43.7 %reduce-scatter.25.cloned.1.call-start = ((), (), s32[]{:S(2)}) async-start(), calls=%async_computation.17 | async-start | bytes 655360 | tf_op jit(solution)/shard_map/reduce_scatter | solution.py:231
  338.7 92.1 %reduce-scatter.29.cloned.1.call-start = ((), (), s32[]{:S(2)}) async-start(), calls=%async_computation.19 | async-start | bytes 655360 | tf_op jit(solution)/shard_map/reduce_scatter | solution.py:97
  380.9 7.5 %collective-permute-start.9 = (bf16[128,768]{0,1:T(8,128)(2,1)S(1)}, bf16[128,768]{0,1:T(8,128)(2,1)S(1)}, u32[]{:S(2)}, u32[]{:S(2)}) collective-permute-start(bf16[128,768]{0,1:T(8,128)(2,1)S(1)} %bitcast.88), channel_id=1, source_target_pairs={{0,1},{1,2},{2,3},{3,0},{4,5},{5,6},{6,7},{7,4},{8,9},{9,10},{10,1... | collective-permute-start | bytes 589832 | tf_op jit(solution)/shard_map/ppermute | solution.py:23
  388.4 7.5 %collective-permute-start.10 = (bf16[128,768]{0,1:T(8,128)(2,1)S(1)}, bf16[128,768]{0,1:T(8,128)(2,1)S(1)}, u32[]{:S(2)}, u32[]{:S(2)}) collective-permute-start(bf16[128,768]{0,1:T(8,128)(2,1)S(1)} %collective-permute-done.9), channel_id=1, source_target_pairs={{0,1},{1,2},{2,3},{3,0},{4,5},{5,6},{6,7},{7,4},{8,9},{9,10},{10,1... | collective-permute-start | bytes 589832 | tf_op jit(solution)/shard_map/ppermute | solution.py:23
  395.8 7.5 %collective-permute-start.11 = (bf16[128,768]{0,1:T(8,128)(2,1)S(1)}, bf16[128,768]{0,1:T(8,128)(2,1)S(1)}, u32[]{:S(2)}, u32[]{:S(2)}) collective-permute-start(bf16[128,768]{0,1:T(8,128)(2,1)S(1)} %collective-permute-done.10), channel_id=1, source_target_pairs={{0,1},{1,2},{2,3},{3,0},{4,5},{5,6},{6,7},{7,4},{8,9},{9,10},{10,1... | collective-permute-start | bytes 589832 | tf_op jit(solution)/shard_map/ppermute | solution.py:23
  405.7 109.7 %all-reduce.9.cloned.1.call-start = ((), (), s32[]{:S(2)}) async-start(), calls=%async_computation.20 | async-start | bytes 6291456 | tf_op jit(solution)/shard_map/psum | solution.py:245
  411.9 29.8 %copy-start.31 = (f32[256]{0:T(256)S(1)}, f32[256]{0:T(256)}, u32[]{:S(2)}) copy-start(f32[256]{0:T(256)} %get-tuple-element.108) | copy-start | bytes 3076
  411.9 29.8 %copy-start.32 = (f32[256]{0:T(256)S(1)}, f32[256]{0:T(256)}, u32[]{:S(2)}) copy-start(f32[256]{0:T(256)} %get-tuple-element.116) | copy-start | bytes 3076
  412.0 42.8 %copy-start.16 = (f32[128,256]{1,0:T(8,128)S(1)}, f32[128,256]{1,0:T(8,128)}, u32[]{:S(2)}) copy-start(f32[128,256]{1,0:T(8,128)} %copy-done.15) | copy-start | bytes 393220
  (28 other events, 322.6 us)
Sparse Core Ops, SparseCore 0:
  31.9 33.6 reduce-scatter.10
  115.2 19.6 reduce-scatter.12
  137.2 43.6 reduce-scatter.18
  183.1 42.7 reduce-scatter.14
  257.8 19.7 reduce-scatter.20
  280.5 21.6 reduce-scatter.16
  312.0 21.8 reduce-scatter.22
  336.8 20.1 reduce-scatter.26
  359.8 20.0 reduce-scatter.24
  405.8 19.7 reduce-scatter.28
  429.2 86.1 all-reduce.8
